TPU v7x, 128 devices: a whole 4x4x4 slice. The times are simulated.
128 devices in a mesh: lat: 8 (over x, core), lon: 16 (over z, y).
Axes of the slice: x: 4, y: 4, z: 4, core: 2. Of those that a mesh axis runs over, the one named last changes fastest.
Arguments:
- prognostic_samples: float32 [40, 25, 64, 2048], P(None, None, 'lat', 'lon'), may hold values from -6 to 6
- wind: float32 [2, 64, 2048], P(None, 'lat', 'lon'), may hold values from -0.4 to 0.4
- obs_lat: int32 [2, 512], replicated, may hold values from 0 to 63
- obs_lon: int32 [2, 512], replicated, may hold values from 0 to 2047
- obs_var: int32 [2, 512], replicated, may hold values from 0 to 24
- obs_value: float32 [2, 512], replicated, may hold values from -6 to 6
- obs_error: float32 [2, 512], replicated, may hold values from 0.5 to 4
Outputs:
- analysis: float32 [40, 25, 64, 2048], P(None, None, 'lat', 'lon')
All inputs are finite; a program needn't handle non-finite values.
Results may differ from a plain program's by a relative error of at most 0.0001.
Values sent between devices are 32-bit elements; how exact they have to be, the bound alone decides.
A program may use at most 128 MiB of HBM per device.

v0:
```python
import jax
import jax.numpy as jnp
from jax import lax
from jax.sharding import PartitionSpec as P

STEPS = 2
BLOCK = 128
HIGHEST = lax.Precision.HIGHEST
DIFFUSE = 0.1


def with_halo(block, sides, width):
    for axis, dim in sides:
        count = lax.axis_size(axis)
        forward = [(i, i + 1) for i in range(count - 1)]
        forward.append((count - 1, 0))
        backward = [(target, source) for source, target in forward]
        low = lax.ppermute(
            lax.slice_in_dim(block, block.shape[dim] - width, None, axis=dim), axis, forward
        )
        high = lax.ppermute(lax.slice_in_dim(block, 0, width, axis=dim), axis, backward)
        block = jnp.concatenate([low, block, high], axis=dim)
    return block


def taper(scaled):
    inner_part = (
        ((-0.25 * scaled + 0.5) * scaled + 0.625) * scaled - 5.0 / 3.0
    ) * scaled * scaled + 1.0
    scaled_safe = jnp.maximum(scaled, 1.0)
    outer_part = (
        ((((scaled / 12.0 - 0.5) * scaled + 0.625) * scaled + 5.0 / 3.0) * scaled - 5.0) * scaled
        + 4.0
        - 2.0 / (3.0 * scaled_safe)
    )
    return jnp.where(scaled <= 1.0, inner_part, jnp.where(scaled < 2.0, outer_part, 0.0))


def taper_to(lat_a, lon_a, lat_b, lon_b, cycle_length, reach):
    meridional_spacing = (lat_a - lat_b).astype(jnp.float32)
    lon_gap = jnp.abs(lon_a - lon_b)
    lon_gap = jnp.minimum(lon_gap, cycle_length - lon_gap).astype(jnp.float32)
    return taper(jnp.sqrt(meridional_spacing * meridional_spacing + lon_gap * lon_gap) / reach)


def advance(padded, east_wind, north_wind):
    centre = padded[..., 1:-1, 1:-1]
    above_v = padded[..., 2:, 1:-1]
    below_v = padded[..., :-2, 1:-1]
    right_v = padded[..., 1:-1, 2:]
    left_v = padded[..., 1:-1, :-2]
    return (
        centre
        - 0.5 * east_wind * (right_v - left_v)
        - 0.5 * north_wind * (above_v - below_v)
        + DIFFUSE * (right_v + left_v + above_v + below_v - 4.0 * centre)
    )


def zero_outside_block(padded, margin):
    overall_line_count = padded.shape[-2]
    band_rows = overall_line_count - 2 * margin
    global_row = (
        lax.axis_index("lat") * band_rows - margin + lax.iota(jnp.int32, overall_line_count)
    )
    inside = (global_row >= 0) & (global_row < band_rows * lax.axis_size("lat"))
    return jnp.where(inside[:, None], padded, 0.0)


def gains(prior, values, errors):
    members = prior.shape[0]
    average = jnp.mean(prior, axis=0)
    anomaly = prior - average
    ensemble_spread = jnp.sum(anomaly * anomaly, axis=0) / (members - 1)
    total = ensemble_spread + errors
    weights = anomaly / ((members - 1) * total)
    shifts = values - average - anomaly / (1.0 + jnp.sqrt(errors / total))
    return (weights, shifts)


def read_priors(sample_realizations, sel_lat, sel_lon, sel_var, band_rows, band_cols):
    members, variables, cells = sample_realizations.shape
    local_lat = sel_lat - lax.axis_index("lat") * band_rows
    local_lon = sel_lon - lax.axis_index("lon") * band_cols
    owned = (local_lat >= 0) & (local_lat < band_rows) & (local_lon >= 0) & (local_lon < band_cols)
    position = (
        sel_var * cells
        + jnp.clip(local_lat, 0, band_rows - 1) * band_cols
        + jnp.clip(local_lon, 0, band_cols - 1)
    )
    picked = jnp.take(sample_realizations.reshape(members, variables * cells), position, axis=1)
    return jnp.where(owned[None, :], picked, 0.0)


def apply_block(sample_realizations, weights, shifts, damping_factors):
    projected = jnp.einsum("mvc,mk->vck", sample_realizations, weights, precision=HIGHEST)
    return sample_realizations + jnp.einsum(
        "vck,mk->mvc", projected * damping_factors, shifts, precision=HIGHEST
    )


def body(prognostic_samples, wind, obs_lat, obs_lon, obs_var, obs_value, obs_error):
    members, variables, band_rows, band_cols = prognostic_samples.shape
    state_now = prognostic_samples
    for section in range(STEPS):
        padded = with_halo(state_now, (("lat", 2), ("lon", 3)), 1)
        state_now = advance(zero_outside_block(padded, 1), wind[0], wind[1])
    sample_realizations = state_now.reshape(members, variables, band_rows * band_cols)
    cycle_length = band_cols * lax.axis_size("lon")
    reach = float(band_rows * lax.axis_size("lat") // 2)
    cell_ids = lax.iota(jnp.int32, band_rows * band_cols)
    cell_lat = (lax.axis_index("lat") * band_rows + cell_ids // band_cols)[:, None]
    cell_lon = (lax.axis_index("lon") * band_cols + cell_ids % band_cols)[:, None]
    block_count = obs_lat.shape[1] // BLOCK
    for batch_no in range(obs_lat.shape[0]):
        sel_lat = obs_lat[batch_no]
        sel_lon = obs_lon[batch_no]
        sel_var = obs_var[batch_no]
        values = obs_value[batch_no]
        errors = obs_error[batch_no]

        def block_slice(array, first_obs):
            return lax.dynamic_slice_in_dim(array, first_obs, BLOCK)

        def single_block(block_no, members_now):
            first_obs = block_no * BLOCK
            blk_lat = block_slice(sel_lat, first_obs)
            block_longitude = block_slice(sel_lon, first_obs)
            own_part = read_priors(
                members_now,
                blk_lat,
                block_longitude,
                block_slice(sel_var, first_obs),
                band_rows,
                band_cols,
            )
            prior = lax.psum(own_part, ("lat", "lon"))
            weights, shifts = gains(
                prior, block_slice(values, first_obs), block_slice(errors, first_obs)
            )
            damping_factors = taper_to(
                cell_lat, cell_lon, blk_lat[None, :], block_longitude[None, :], cycle_length, reach
            )
            return apply_block(members_now, weights, shifts, damping_factors)

        sample_realizations = lax.fori_loop(0, block_count, single_block, sample_realizations)
    return sample_realizations.reshape(members, variables, band_rows, band_cols)


def solution(mesh):
    in_specs = (P(None, None, "lat", "lon"), P(None, "lat", "lon"), P(), P(), P(), P(), P())
    out_specs = P(None, None, "lat", "lon")
    return jax.shard_map(body, mesh=mesh, in_specs=in_specs, out_specs=out_specs, check_vma=False)
```

profile of v0, /device:TPU:1, one launch (start us, length us, event | category | flops | bytes accessed | tf_op | source)
XLA Modules:
  0.0 1001.6 jit_solution(13554984503513488470)
XLA Ops:
  7.6 9.6 copy.111
  44.0 15.4 %copy.114 = f32[40,25,10,128]{3,0,2,1:T(8,128)} copy(f32[40,25,10,128]{0,1,3,2:T(8,128)} %copy-done) | data formatting | bytes 10240000 | tf_op jit(solution)/shard_map/concatenate | solution.py:22
  66.1 13.4 %maximum_select_fusion = f32[40,25,10,130]{3,0,2,1:T(8,128)} fusion(f32[40,25,10,1]{3,0,2,1:T(8,128)} %copy.115, f32[40,25,10,128]{3,0,2,1:T(8,128)} %copy.114, f32[40,25,10,1]{3,0,2,1:T(8,128)} %copy.113, pred[10]{0:T(512)(128)(4,1)S(1)} %compare_and_fusion.4), kind=kLoop, calls=%fused_computation.101 | loop fusion | flops 3900000 | bytes 10400010 | tf_op jit(solution)/shard_map/jit(_where)/select_n | solution.py:67
  79.4 14.2 %multiply_add_fusion.2 = f32[40,25,8,128]{3,0,2,1:T(8,128)S(1)} fusion(f32[40,25,10,130]{3,0,2,1:T(8,128)} %maximum_select_fusion, f32[8,128]{1,0:T(8,128)S(1)} %get-tuple-element.578, f32[8,128]{1,0:T(8,128)S(1)} %get-tuple-element.577), kind=kLoop, calls=%fused_computation.106 | loop fusion | flops 13312000 | bytes 24584192 | tf_op jit(solution)/shard_map/add | solution.py:53
  118.7 17.7 %collective-permute-start.7 = (f32[40,25,10,1]{0,1,3,2:T(8,128)S(1)}, f32[40,25,10,1]{0,1,3,2:T(8,128)S(1)}, u32[]{:S(2)}, u32[]{:S(2)}) collective-permute-start(f32[40,25,10,1]{0,1,3,2:T(8,128)S(1)} %copy.127), channel_id=1, source_target_pairs={{1,0},{2,1},{3,2},{4,3},{5,4},{6,5},{7,6},{8,7},{9,8},{10,9},{11,1... | collective-permute-start | bytes 120008 | tf_op jit(solution)/shard_map/ppermute | solution.py:21
  143.1 9.6 maximum_select_fusion.1
  158.4 420.0 %while.32 = (s32[]{:T(128)}, f32[40,25,1024]{2,0,1:T(8,128)}, f32[512]{0:T(512)S(1)}, s32[512]{0:T(512)S(1)}, s32[512]{0:T(512)S(1)}, /*index=5*/s32[512]{0:T(51...) while((s32[]{:T(128)}, f32[40,25,1024]{2,0,1:T(8,128)}, ...), condition=%wide.region_4.6_spmd.clone, body=%wide.region_0.5_spmd.clone.sunk | while | flops 3155089920 | bytes 48024392 | solution.py:146
  173.2 67.1 %psum.32 = f32[40,128]{1,0:T(8,128)S(1)} all-reduce(f32[40,128]{1,0:T(8,128)S(1)} %bitcast_select_fusion.4), channel_id=1, replica_groups=mesh['lat'=8,'lon'=16] {'lat','lon'}, use_global_device_ids=true, to_apply=%region_1.2 | all-reduce | flops 5120 | bytes 40960 | tf_op jit(solution)/shard_map/while/body/eval_jaxpr/psum | solution.py:137
  240.5 14.2 %fusion.86 = f32[128,25,1024]{2,0,1:T(8,128)S(1)} fusion(f32[40,25,1024]{2,0,1:T(8,128)} %get-tuple-element.762, f32[40,128]{1,0:T(8,128)S(1)} %psum.32, f32[128]{0:T(128)S(1)} %get-tuple-element.718, f32[128]{0:T(128)S(1)} %get-tuple-element.717), kind=kOutput, calls=%fused_computation.22.clone.1 | convolution fusion | flops 1572874240 | bytes 17224704 | tf_op jit(solution)/shard_map/while/body/eval_jaxpr/mvc,mk->vck/dot_general | solution.py:96
  255.7 10.6 %fusion.89 = f32[40,25,1024]{2,0,1:T(8,128)} fusion(f32[40,25,1024]{2,0,1:T(8,128)} %get-tuple-element.762, f32[128,25,1024]{2,0,1:T(8,128)S(1)} %fusion.86, f32[1024,128]{0,1:T(8,128)S(1)} %fusion.88, f32[40,128]{1,0:T(8,128)S(1)} %psum.32, f32[128]{0:T(128)S(1)} %get-tuple-element.721, f32[128]{0:T(128)S(1)} %get-tuple-element.717, ...), kind=kOutput, calls=%fused_computation.9.clone.1 | convolution fusion | flops 1577180160 | bytes 21845504 | tf_op jit(solution)/shard_map/while/body/eval_jaxpr/vck,mk->mvc/dot_general | solution.py:97
  281.1 63.1 %psum.32 = f32[40,128]{1,0:T(8,128)S(1)} all-reduce(f32[40,128]{1,0:T(8,128)S(1)} %bitcast_select_fusion.4), channel_id=1, replica_groups=mesh['lat'=8,'lon'=16] {'lat','lon'}, use_global_device_ids=true, to_apply=%region_1.2 | all-reduce | flops 5120 | bytes 40960 | tf_op jit(solution)/shard_map/while/body/eval_jaxpr/psum | solution.py:137
  344.4 14.2 %fusion.86 = f32[128,25,1024]{2,0,1:T(8,128)S(1)} fusion(f32[40,25,1024]{2,0,1:T(8,128)} %get-tuple-element.762, f32[40,128]{1,0:T(8,128)S(1)} %psum.32, f32[128]{0:T(128)S(1)} %get-tuple-element.718, f32[128]{0:T(128)S(1)} %get-tuple-element.717), kind=kOutput, calls=%fused_computation.22.clone.1 | convolution fusion | flops 1572874240 | bytes 17224704 | tf_op jit(solution)/shard_map/while/body/eval_jaxpr/mvc,mk->vck/dot_general | solution.py:96
  359.5 10.6 %fusion.89 = f32[40,25,1024]{2,0,1:T(8,128)} fusion(f32[40,25,1024]{2,0,1:T(8,128)} %get-tuple-element.762, f32[128,25,1024]{2,0,1:T(8,128)S(1)} %fusion.86, f32[1024,128]{0,1:T(8,128)S(1)} %fusion.88, f32[40,128]{1,0:T(8,128)S(1)} %psum.32, f32[128]{0:T(128)S(1)} %get-tuple-element.721, f32[128]{0:T(128)S(1)} %get-tuple-element.717, ...), kind=kOutput, calls=%fused_computation.9.clone.1 | convolution fusion | flops 1577180160 | bytes 21845504 | tf_op jit(solution)/shard_map/while/body/eval_jaxpr/vck,mk->mvc/dot_general | solution.py:97
  384.9 64.0 %psum.32 = f32[40,128]{1,0:T(8,128)S(1)} all-reduce(f32[40,128]{1,0:T(8,128)S(1)} %bitcast_select_fusion.4), channel_id=1, replica_groups=mesh['lat'=8,'lon'=16] {'lat','lon'}, use_global_device_ids=true, to_apply=%region_1.2 | all-reduce | flops 5120 | bytes 40960 | tf_op jit(solution)/shard_map/while/body/eval_jaxpr/psum | solution.py:137
  449.1 14.2 %fusion.86 = f32[128,25,1024]{2,0,1:T(8,128)S(1)} fusion(f32[40,25,1024]{2,0,1:T(8,128)} %get-tuple-element.762, f32[40,128]{1,0:T(8,128)S(1)} %psum.32, f32[128]{0:T(128)S(1)} %get-tuple-element.718, f32[128]{0:T(128)S(1)} %get-tuple-element.717), kind=kOutput, calls=%fused_computation.22.clone.1 | convolution fusion | flops 1572874240 | bytes 17224704 | tf_op jit(solution)/shard_map/while/body/eval_jaxpr/mvc,mk->vck/dot_general | solution.py:96
  464.3 10.6 %fusion.89 = f32[40,25,1024]{2,0,1:T(8,128)} fusion(f32[40,25,1024]{2,0,1:T(8,128)} %get-tuple-element.762, f32[128,25,1024]{2,0,1:T(8,128)S(1)} %fusion.86, f32[1024,128]{0,1:T(8,128)S(1)} %fusion.88, f32[40,128]{1,0:T(8,128)S(1)} %psum.32, f32[128]{0:T(128)S(1)} %get-tuple-element.721, f32[128]{0:T(128)S(1)} %get-tuple-element.717, ...), kind=kOutput, calls=%fused_computation.9.clone.1 | convolution fusion | flops 1577180160 | bytes 21845504 | tf_op jit(solution)/shard_map/while/body/eval_jaxpr/vck,mk->mvc/dot_general | solution.py:97
  489.6 62.8 %psum.32 = f32[40,128]{1,0:T(8,128)S(1)} all-reduce(f32[40,128]{1,0:T(8,128)S(1)} %bitcast_select_fusion.4), channel_id=1, replica_groups=mesh['lat'=8,'lon'=16] {'lat','lon'}, use_global_device_ids=true, to_apply=%region_1.2 | all-reduce | flops 5120 | bytes 40960 | tf_op jit(solution)/shard_map/while/body/eval_jaxpr/psum | solution.py:137
  552.7 14.2 %fusion.86 = f32[128,25,1024]{2,0,1:T(8,128)S(1)} fusion(f32[40,25,1024]{2,0,1:T(8,128)} %get-tuple-element.762, f32[40,128]{1,0:T(8,128)S(1)} %psum.32, f32[128]{0:T(128)S(1)} %get-tuple-element.718, f32[128]{0:T(128)S(1)} %get-tuple-element.717), kind=kOutput, calls=%fused_computation.22.clone.1 | convolution fusion | flops 1572874240 | bytes 17224704 | tf_op jit(solution)/shard_map/while/body/eval_jaxpr/mvc,mk->vck/dot_general | solution.py:96
  567.8 10.6 %fusion.89 = f32[40,25,1024]{2,0,1:T(8,128)} fusion(f32[40,25,1024]{2,0,1:T(8,128)} %get-tuple-element.762, f32[128,25,1024]{2,0,1:T(8,128)S(1)} %fusion.86, f32[1024,128]{0,1:T(8,128)S(1)} %fusion.88, f32[40,128]{1,0:T(8,128)S(1)} %psum.32, f32[128]{0:T(128)S(1)} %get-tuple-element.721, f32[128]{0:T(128)S(1)} %get-tuple-element.717, ...), kind=kOutput, calls=%fused_computation.9.clone.1 | convolution fusion | flops 1577180160 | bytes 21845504 | tf_op jit(solution)/shard_map/while/body/eval_jaxpr/vck,mk->mvc/dot_general | solution.py:97
  578.5 417.4 %while.33 = (s32[]{:T(128)}, f32[40,25,1024]{2,0,1:T(8,128)}, f32[512]{0:T(512)S(1)}, s32[512]{0:T(512)S(1)}, s32[512]{0:T(512)S(1)}, /*index=5*/s32[512]{0:T(51...) while((s32[]{:T(128)}, f32[40,25,1024]{2,0,1:T(8,128)}, ...), condition=%wide.region_9.11_spmd.clone, body=%wide.region_5.10_spmd.clone.sunk | while | flops 3155089920 | bytes 48024392 | solution.py:146
  593.4 64.3 %psum.33 = f32[40,128]{1,0:T(8,128)S(1)} all-reduce(f32[40,128]{1,0:T(8,128)S(1)} %bitcast_select_fusion.5), channel_id=1, replica_groups=mesh['lat'=8,'lon'=16] {'lat','lon'}, use_global_device_ids=true, to_apply=%region_6.7 | all-reduce | flops 5120 | bytes 40960 | tf_op jit(solution)/shard_map/while/body/eval_jaxpr/psum | solution.py:137
  657.9 14.2 %fusion.93 = f32[128,25,1024]{2,0,1:T(8,128)S(1)} fusion(f32[40,25,1024]{2,0,1:T(8,128)} %get-tuple-element.816, f32[40,128]{1,0:T(8,128)S(1)} %psum.33, f32[128]{0:T(128)S(1)} %get-tuple-element.738, f32[128]{0:T(128)S(1)} %get-tuple-element.737), kind=kOutput, calls=%fused_computation.69.clone.1 | convolution fusion | flops 1572874240 | bytes 17224704 | tf_op jit(solution)/shard_map/while/body/eval_jaxpr/mvc,mk->vck/dot_general | solution.py:96
  673.1 10.6 %fusion.96 = f32[40,25,1024]{2,0,1:T(8,128)} fusion(f32[40,25,1024]{2,0,1:T(8,128)} %get-tuple-element.816, f32[128,25,1024]{2,0,1:T(8,128)S(1)} %fusion.93, f32[1024,128]{0,1:T(8,128)S(1)} %fusion.95, f32[40,128]{1,0:T(8,128)S(1)} %psum.33, f32[128]{0:T(128)S(1)} %get-tuple-element.741, f32[128]{0:T(128)S(1)} %get-tuple-element.737, ...), kind=kOutput, calls=%fused_computation.56.clone.1 | convolution fusion | flops 1577180160 | bytes 21845504 | tf_op jit(solution)/shard_map/while/body/eval_jaxpr/vck,mk->mvc/dot_general | solution.py:97
  698.5 62.8 %psum.33 = f32[40,128]{1,0:T(8,128)S(1)} all-reduce(f32[40,128]{1,0:T(8,128)S(1)} %bitcast_select_fusion.5), channel_id=1, replica_groups=mesh['lat'=8,'lon'=16] {'lat','lon'}, use_global_device_ids=true, to_apply=%region_6.7 | all-reduce | flops 5120 | bytes 40960 | tf_op jit(solution)/shard_map/while/body/eval_jaxpr/psum | solution.py:137
  761.5 14.2 %fusion.93 = f32[128,25,1024]{2,0,1:T(8,128)S(1)} fusion(f32[40,25,1024]{2,0,1:T(8,128)} %get-tuple-element.816, f32[40,128]{1,0:T(8,128)S(1)} %psum.33, f32[128]{0:T(128)S(1)} %get-tuple-element.738, f32[128]{0:T(128)S(1)} %get-tuple-element.737), kind=kOutput, calls=%fused_computation.69.clone.1 | convolution fusion | flops 1572874240 | bytes 17224704 | tf_op jit(solution)/shard_map/while/body/eval_jaxpr/mvc,mk->vck/dot_general | solution.py:96
  776.7 10.6 %fusion.96 = f32[40,25,1024]{2,0,1:T(8,128)} fusion(f32[40,25,1024]{2,0,1:T(8,128)} %get-tuple-element.816, f32[128,25,1024]{2,0,1:T(8,128)S(1)} %fusion.93, f32[1024,128]{0,1:T(8,128)S(1)} %fusion.95, f32[40,128]{1,0:T(8,128)S(1)} %psum.33, f32[128]{0:T(128)S(1)} %get-tuple-element.741, f32[128]{0:T(128)S(1)} %get-tuple-element.737, ...), kind=kOutput, calls=%fused_computation.56.clone.1 | convolution fusion | flops 1577180160 | bytes 21845504 | tf_op jit(solution)/shard_map/while/body/eval_jaxpr/vck,mk->mvc/dot_general | solution.py:97
  802.0 64.3 %psum.33 = f32[40,128]{1,0:T(8,128)S(1)} all-reduce(f32[40,128]{1,0:T(8,128)S(1)} %bitcast_select_fusion.5), channel_id=1, replica_groups=mesh['lat'=8,'lon'=16] {'lat','lon'}, use_global_device_ids=true, to_apply=%region_6.7 | all-reduce | flops 5120 | bytes 40960 | tf_op jit(solution)/shard_map/while/body/eval_jaxpr/psum | solution.py:137
  866.5 14.2 %fusion.93 = f32[128,25,1024]{2,0,1:T(8,128)S(1)} fusion(f32[40,25,1024]{2,0,1:T(8,128)} %get-tuple-element.816, f32[40,128]{1,0:T(8,128)S(1)} %psum.33, f32[128]{0:T(128)S(1)} %get-tuple-element.738, f32[128]{0:T(128)S(1)} %get-tuple-element.737), kind=kOutput, calls=%fused_computation.69.clone.1 | convolution fusion | flops 1572874240 | bytes 17224704 | tf_op jit(solution)/shard_map/while/body/eval_jaxpr/mvc,mk->vck/dot_general | solution.py:96
  881.7 10.6 %fusion.96 = f32[40,25,1024]{2,0,1:T(8,128)} fusion(f32[40,25,1024]{2,0,1:T(8,128)} %get-tuple-element.816, f32[128,25,1024]{2,0,1:T(8,128)S(1)} %fusion.93, f32[1024,128]{0,1:T(8,128)S(1)} %fusion.95, f32[40,128]{1,0:T(8,128)S(1)} %psum.33, f32[128]{0:T(128)S(1)} %get-tuple-element.741, f32[128]{0:T(128)S(1)} %get-tuple-element.737, ...), kind=kOutput, calls=%fused_computation.56.clone.1 | convolution fusion | flops 1577180160 | bytes 21845504 | tf_op jit(solution)/shard_map/while/body/eval_jaxpr/vck,mk->mvc/dot_general | solution.py:97
  907.1 62.8 %psum.33 = f32[40,128]{1,0:T(8,128)S(1)} all-reduce(f32[40,128]{1,0:T(8,128)S(1)} %bitcast_select_fusion.5), channel_id=1, replica_groups=mesh['lat'=8,'lon'=16] {'lat','lon'}, use_global_device_ids=true, to_apply=%region_6.7 | all-reduce | flops 5120 | bytes 40960 | tf_op jit(solution)/shard_map/while/body/eval_jaxpr/psum | solution.py:137
  970.1 14.2 %fusion.93 = f32[128,25,1024]{2,0,1:T(8,128)S(1)} fusion(f32[40,25,1024]{2,0,1:T(8,128)} %get-tuple-element.816, f32[40,128]{1,0:T(8,128)S(1)} %psum.33, f32[128]{0:T(128)S(1)} %get-tuple-element.738, f32[128]{0:T(128)S(1)} %get-tuple-element.737), kind=kOutput, calls=%fused_computation.69.clone.1 | convolution fusion | flops 1572874240 | bytes 17224704 | tf_op jit(solution)/shard_map/while/body/eval_jaxpr/mvc,mk->vck/dot_general | solution.py:96
  985.3 10.6 %fusion.96 = f32[40,25,1024]{2,0,1:T(8,128)} fusion(f32[40,25,1024]{2,0,1:T(8,128)} %get-tuple-element.816, f32[128,25,1024]{2,0,1:T(8,128)S(1)} %fusion.93, f32[1024,128]{0,1:T(8,128)S(1)} %fusion.95, f32[40,128]{1,0:T(8,128)S(1)} %psum.33, f32[128]{0:T(128)S(1)} %get-tuple-element.741, f32[128]{0:T(128)S(1)} %get-tuple-element.737, ...), kind=kOutput, calls=%fused_computation.56.clone.1 | convolution fusion | flops 1577180160 | bytes 21845504 | tf_op jit(solution)/shard_map/while/body/eval_jaxpr/vck,mk->mvc/dot_general | solution.py:97
  (161 shorter events, 210.7 us)
Async XLA Ops:
  4.2 13.1 %collective-permute-start = (f32[40,25,1,128]{3,0,2,1:T(8,128)S(1)}, f32[40,25,1,128]{3,0,2,1:T(8,128)S(1)}, u32[]{:S(2)}, u32[]{:S(2)}) collective-permute-start(f32[40,25,1,128]{3,0,2,1:T(8,128)S(1)} %copy.124), channel_id=1, source_target_pairs={{0,16},{16,32},{32,48},{48,64},{64,80},{80,96},{96,112},{112,0},{1... | collective-permute-start | bytes 1536008 | tf_op jit(solution)/shard_map/ppermute | solution.py:18
  7.6 9.6 copy-start.3
  7.6 9.6 copy-start.2
  7.6 11.5 %collective-permute-start.1 = (f32[40,25,1,128]{3,0,2,1:T(8,128)}, f32[40,25,1,128]{3,0,2,1:T(8,128)S(1)}, u32[]{:S(2)}, u32[]{:S(2)}) collective-permute-start(f32[40,25,1,128]{3,0,2,1:T(8,128)} %copy.125), channel_id=1, source_target_pairs={{16,0},{32,16},{48,32},{64,48},{80,64},{96,80},{112,96},{0,112},{1... | collective-permute-start | bytes 1536008 | tf_op jit(solution)/shard_map/ppermute | solution.py:21
  30.4 7.0 copy-start
  37.4 22.0 %collective-permute-start.2 = (f32[40,25,10,1]{0,1,3,2:T(8,128)S(1)}, f32[40,25,10,1]{0,1,3,2:T(8,128)S(1)}, u32[]{:S(2)}, u32[]{:S(2)}) collective-permute-start(f32[40,25,10,1]{0,1,3,2:T(8,128)S(1)} %get-tuple-element.569), channel_id=1, source_target_pairs={{0,1},{1,2},{2,3},{3,4},{4,5},{5,6},{6,7},{7,8},{8,9},{9,10},{10,1... | collective-permute-start | bytes 120008 | tf_op jit(solution)/shard_map/ppermute | solution.py:18
  38.7 24.0 %collective-permute-start.3 = (f32[40,25,10,1]{0,1,3,2:T(8,128)S(1)}, f32[40,25,10,1]{0,1,3,2:T(8,128)S(1)}, u32[]{:S(2)}, u32[]{:S(2)}) collective-permute-start(f32[40,25,10,1]{0,1,3,2:T(8,128)S(1)} %get-tuple-element.570), channel_id=1, source_target_pairs={{1,0},{2,1},{3,2},{4,3},{5,4},{6,5},{7,6},{8,7},{9,8},{10,9},{11,1... | collective-permute-start | bytes 120008 | tf_op jit(solution)/shard_map/ppermute | solution.py:21
  79.4 16.5 %copy-start.4 = (s32[2,512]{1,0:T(2,128)S(1)}, s32[2,512]{1,0:T(2,128)}, u32[]{:S(2)}) copy-start(s32[2,512]{1,0:T(2,128)} %param.15) | copy-start | bytes 12292
  79.4 16.5 %copy-start.5 = (s32[2,512]{1,0:T(2,128)S(1)}, s32[2,512]{1,0:T(2,128)}, u32[]{:S(2)}) copy-start(s32[2,512]{1,0:T(2,128)} %param.16) | copy-start | bytes 12292
  79.4 16.5 %copy-start.6 = (s32[2,512]{1,0:T(2,128)S(1)}, s32[2,512]{1,0:T(2,128)}, u32[]{:S(2)}) copy-start(s32[2,512]{1,0:T(2,128)} %param.17) | copy-start | bytes 12292
  93.7 11.3 %copy-start.1 = (f32[40,25,8,128]{3,0,2,1:T(8,128)}, f32[40,25,8,128]{3,0,2,1:T(8,128)S(1)}, u32[]{:S(2)}) copy-start(f32[40,25,8,128]{3,0,2,1:T(8,128)S(1)} %multiply_add_fusion.2) | copy-start | bytes 12288004
  93.8 8.0 collective-permute-start.4
  95.8 8.8 collective-permute-start.5
  110.5 25.9 %copy-start.7 = (f32[2,512]{1,0:T(2,128)S(1)}, f32[2,512]{1,0:T(2,128)}, u32[]{:S(2)}) copy-start(f32[2,512]{1,0:T(2,128)} %param.19) | copy-start | bytes 12292
  114.6 21.8 %collective-permute-start.6 = (f32[40,25,10,1]{0,1,3,2:T(8,128)S(1)}, f32[40,25,10,1]{0,1,3,2:T(8,128)S(1)}, u32[]{:S(2)}, u32[]{:S(2)}) collective-permute-start(f32[40,25,10,1]{0,1,3,2:T(8,128)S(1)} %copy.126), channel_id=1, source_target_pairs={{0,1},{1,2},{2,3},{3,4},{4,5},{5,6},{6,7},{7,8},{8,9},{9,10},{10,1... | collective-permute-start | bytes 120008 | tf_op jit(solution)/shard_map/ppermute | solution.py:18
  118.7 21.0 %collective-permute-start.7 = (f32[40,25,10,1]{0,1,3,2:T(8,128)S(1)}, f32[40,25,10,1]{0,1,3,2:T(8,128)S(1)}, u32[]{:S(2)}, u32[]{:S(2)}) collective-permute-start(f32[40,25,10,1]{0,1,3,2:T(8,128)S(1)} %copy.127), channel_id=1, source_target_pairs={{1,0},{2,1},{3,2},{4,3},{5,4},{6,5},{7,6},{8,7},{9,8},{10,9},{11,1... | collective-permute-start | bytes 120008 | tf_op jit(solution)/shard_map/ppermute | solution.py:21
where the time goes:
time: 1010 us; the launch traced here: 1000 us
  blocking collectives  511 us (51%)
  matrix products  199 us (20%)
  local copies, waits for them, and re-layouts  190 us (19%)
  other arithmetic  62.4 us (6%)
  starting transfers between devices  29.1 us (3%)
    psum x8, blocking collectives, single_block(): prior = lax.psum(own_part, ('lat', 'lon'))  511 us
    dot_general x8, matrix products, apply_block(): jnp.einsum('mvc,mk->vck', sample_realizations, weights, precision=HIGHEST)  114 us
    dot_general x8, matrix products, apply_block(): jnp.einsum('vck,mk->mvc', projected * damping_factors, shifts, precision=...  84.9 us
    while x8, local copies, waits for them, and re-layouts  73 us
    gather x16, local copies, waits for them, and re-layouts, read_priors(): jnp.take(sample_realizations.reshape(members, variables * cells), positio...  43.4 us
    unnamed x22, local copies, waits for them, and re-layouts  28.7 us
    ppermute x4, starting transfers between devices, with_halo(): lax.ppermute(lax.slice_in_dim(block, 0, width, axis=dim), axis, backward)  23.1 us
    select_n x2, other arithmetic, zero_outside_block(): return jnp.where(inside[:, None], padded, 0.0)  23 us
  transfers between devices with their start and end apart: 8, of which 2 were waited for; matrix products, arithmetic and copies ran while one was open for 4% of the time, Pallas kernels for 0%

commit v1 on v0

--- a/solution.py
+++ b/solution.py
@@ -134,7 +134,8 @@
                 band_rows,
                 band_cols,
             )
-            prior = lax.psum(own_part, ("lat", "lon"))
+            blocks = lax.all_gather(own_part, ("lat", "lon"))
+            prior = jnp.sum(blocks, axis=0)
             weights, shifts = gains(
                 prior, block_slice(values, first_obs), block_slice(errors, first_obs)
             )

time: 1010 us -> 1040 us (1.030)
  blocking collectives: 511 us -> 0 us
  waiting for transfers between devices: 8.6 us -> 510 us
  other arithmetic: 62.4 us -> 88 us
  local copies, waits for them, and re-layouts: 190 us -> 215 us
  between operations: 0.58 us -> 13.9 us
  starting transfers between devices: 29.1 us -> 16.7 us
  matrix products: 199 us -> 188 us
    psum x8 -> x0, blocking collectives: 511 us -> none  [single_block(): prior = lax.psum(own_part, ('lat', 'lon'))]
    all_gather x0 -> x8, waiting for transfers between devices: none -> 501 us  [single_block(): blocks = lax.all_gather(own_part, ('lat', 'lon'))]
    while x8 -> x56, local copies, waits for them, and re-layouts: 73 us -> 92.2 us
    reduce_sum x0 -> x8, other arithmetic: none -> 16.8 us  [single_block(): prior = jnp.sum(blocks, axis=0)]
    ppermute x4, starting transfers between devices: 23.1 us -> 10.6 us  [with_halo(): lax.ppermute(lax.slice_in_dim(block, 0, width, axis=dim), axis, backward)]
    dot_general x8, matrix products: 84.9 us -> 73.4 us  [apply_block(): jnp.einsum('vck,mk->mvc', projected * damping_factors, shifts, precision=...]
    gather x16 -> x8, local copies, waits for them, and re-layouts: 43.4 us -> 43 us  [read_priors(): jnp.take(sample_realizations.reshape(members, variables * cells), positio...]
  transfers between devices with their start and end apart: 8 -> 16, of which waited for: 2 -> 10; matrix products, arithmetic and copies ran while one was open for 4% -> 4% of each run, Pallas kernels for 0% -> 0%
where the time goes in v1:
time: 1040 us; the launch traced here: 1030 us
  waiting for transfers between devices  510 us (49%)
  local copies, waits for them, and re-layouts  215 us (21%)
  matrix products  188 us (18%)
  other arithmetic  88 us (8%)
  starting transfers between devices  16.7 us (2%)
  between operations  13.9 us (1%)
    all_gather x8, waiting for transfers between devices, single_block(): blocks = lax.all_gather(own_part, ('lat', 'lon'))  501 us
    dot_general x8, matrix products, apply_block(): jnp.einsum('mvc,mk->vck', sample_realizations, weights, precision=HIGHEST)  115 us
    while x56, local copies, waits for them, and re-layouts  92.2 us
    dot_general x8, matrix products, apply_block(): jnp.einsum('vck,mk->mvc', projected * damping_factors, shifts, precision=...  73.4 us
    gather x8, local copies, waits for them, and re-layouts, read_priors(): jnp.take(sample_realizations.reshape(members, variables * cells), positio...  43 us
    unnamed x22, local copies, waits for them, and re-layouts  28.7 us
    select_n x2, other arithmetic, zero_outside_block(): return jnp.where(inside[:, None], padded, 0.0)  23 us
  transfers between devices with their start and end apart: 16, of which 10 were waited for; matrix products, arithmetic and copies ran while one was open for 4% of the time, Pallas kernels for 0%

profile of v1, /device:TPU:1, one launch (start us, length us, event | category | flops | bytes accessed | tf_op | source)
XLA Modules:
  0.0 1032.9 jit_solution(5691756345463620665)
XLA Ops:
  14.1 9.6 copy.81
  51.1 15.4 %copy.84 = f32[40,25,10,128]{3,0,2,1:T(8,128)} copy(f32[40,25,10,128]{0,1,3,2:T(8,128)} %copy-done.6) | data formatting | bytes 10240000 | tf_op jit(solution)/shard_map/concatenate | solution.py:22
  73.2 13.4 %maximum_select_fusion = f32[40,25,10,130]{3,0,2,1:T(8,128)} fusion(f32[40,25,10,1]{3,0,2,1:T(8,128)} %copy.85, f32[40,25,10,128]{3,0,2,1:T(8,128)} %copy.84, f32[40,25,10,1]{3,0,2,1:T(8,128)} %copy.83, pred[10]{0:T(512)(128)(4,1)S(1)} %compare_and_fusion.4), kind=kLoop, calls=%fused_computation.101 | loop fusion | flops 3900000 | bytes 10400010 | tf_op jit(solution)/shard_map/jit(_where)/select_n | solution.py:67
  86.6 14.3 %multiply_add_fusion.2 = f32[40,25,8,128]{3,0,2,1:T(8,128)S(1)} fusion(f32[40,25,10,130]{3,0,2,1:T(8,128)} %maximum_select_fusion, f32[8,128]{1,0:T(8,128)S(1)} %get-tuple-element.578, f32[8,128]{1,0:T(8,128)S(1)} %get-tuple-element.577), kind=kLoop, calls=%fused_computation.106 | loop fusion | flops 13312000 | bytes 24584192 | tf_op jit(solution)/shard_map/add | solution.py:53
  137.9 9.6 maximum_select_fusion.1
  153.3 434.3 %while.32 = (s32[]{:T(128)}, f32[40,25,1024]{2,0,1:T(8,128)}, f32[512]{0:T(512)S(1)}, s32[512]{0:T(512)S(1)}, s32[512]{0:T(512)S(1)}, /*index=5*/s32[512]{0:T(51...) while((s32[]{:T(128)}, f32[40,25,1024]{2,0,1:T(8,128)}, ...), condition=%wide.region_4.6_spmd.clone, body=%wide.region_0.5_spmd.clone.sunk | while | flops 3156385280 | bytes 104405952 | solution.py:147
  169.9 66.3 %all-gather.11.cloned.1.call-done = f32[5120,128]{1,0:T(8,128)} async-done(((f32[40,128]{1,0:T(8,128)}), f32[5120,128]{1,0:T(8,128)}) %all-gather.11.cloned.1.call-update) | async-done | bytes 2621456 | tf_op jit(solution)/shard_map/while/body/eval_jaxpr/all_gather | solution.py:137
  239.7 14.4 %fusion.86 = f32[128,25,1024]{2,0,1:T(8,128)S(1)} fusion(f32[40,25,1024]{2,0,1:T(8,128)} %get-tuple-element.762, f32[40,128]{1,0:T(8,128)S(1)} %reduce_sum.111, f32[128]{0:T(128)S(1)} %get-tuple-element.718, f32[128]{0:T(128)S(1)} %get-tuple-element.717), kind=kOutput, calls=%fused_computation.23.clone.1 | convolution fusion | flops 1572874240 | bytes 17224704 | tf_op jit(solution)/shard_map/while/body/eval_jaxpr/mvc,mk->vck/dot_general | solution.py:96
  254.1 9.2 fusion.89
  265.4 9.1 copy.105
  281.6 62.1 %all-gather.11.cloned.1.call-done = f32[5120,128]{1,0:T(8,128)} async-done(((f32[40,128]{1,0:T(8,128)}), f32[5120,128]{1,0:T(8,128)}) %all-gather.11.cloned.1.call-update) | async-done | bytes 2621456 | tf_op jit(solution)/shard_map/while/body/eval_jaxpr/all_gather | solution.py:137
  347.1 14.4 %fusion.86 = f32[128,25,1024]{2,0,1:T(8,128)S(1)} fusion(f32[40,25,1024]{2,0,1:T(8,128)} %get-tuple-element.762, f32[40,128]{1,0:T(8,128)S(1)} %reduce_sum.111, f32[128]{0:T(128)S(1)} %get-tuple-element.718, f32[128]{0:T(128)S(1)} %get-tuple-element.717), kind=kOutput, calls=%fused_computation.23.clone.1 | convolution fusion | flops 1572874240 | bytes 17224704 | tf_op jit(solution)/shard_map/while/body/eval_jaxpr/mvc,mk->vck/dot_general | solution.py:96
  361.5 9.2 fusion.89
  389.1 62.1 %all-gather.11.cloned.1.call-done = f32[5120,128]{1,0:T(8,128)} async-done(((f32[40,128]{1,0:T(8,128)}), f32[5120,128]{1,0:T(8,128)}) %all-gather.11.cloned.1.call-update) | async-done | bytes 2621456 | tf_op jit(solution)/shard_map/while/body/eval_jaxpr/all_gather | solution.py:137
  454.6 14.4 %fusion.86 = f32[128,25,1024]{2,0,1:T(8,128)S(1)} fusion(f32[40,25,1024]{2,0,1:T(8,128)} %get-tuple-element.762, f32[40,128]{1,0:T(8,128)S(1)} %reduce_sum.111, f32[128]{0:T(128)S(1)} %get-tuple-element.718, f32[128]{0:T(128)S(1)} %get-tuple-element.717), kind=kOutput, calls=%fused_computation.23.clone.1 | convolution fusion | flops 1572874240 | bytes 17224704 | tf_op jit(solution)/shard_map/while/body/eval_jaxpr/mvc,mk->vck/dot_general | solution.py:96
  469.0 9.2 fusion.89
  496.5 62.1 %all-gather.11.cloned.1.call-done = f32[5120,128]{1,0:T(8,128)} async-done(((f32[40,128]{1,0:T(8,128)}), f32[5120,128]{1,0:T(8,128)}) %all-gather.11.cloned.1.call-update) | async-done | bytes 2621456 | tf_op jit(solution)/shard_map/while/body/eval_jaxpr/all_gather | solution.py:137
  562.0 14.4 %fusion.86 = f32[128,25,1024]{2,0,1:T(8,128)S(1)} fusion(f32[40,25,1024]{2,0,1:T(8,128)} %get-tuple-element.762, f32[40,128]{1,0:T(8,128)S(1)} %reduce_sum.111, f32[128]{0:T(128)S(1)} %get-tuple-element.718, f32[128]{0:T(128)S(1)} %get-tuple-element.717), kind=kOutput, calls=%fused_computation.23.clone.1 | convolution fusion | flops 1572874240 | bytes 17224704 | tf_op jit(solution)/shard_map/while/body/eval_jaxpr/mvc,mk->vck/dot_general | solution.py:96
  576.4 9.2 fusion.89
  587.6 432.7 %while.33 = (s32[]{:T(128)}, f32[40,25,1024]{2,0,1:T(8,128)}, f32[512]{0:T(512)}, s32[512]{0:T(512)S(1)}, s32[512]{0:T(512)S(1)}, /*index=5*/s32[512]{0:T(512)S(...) while((s32[]{:T(128)}, f32[40,25,1024]{2,0,1:T(8,128)}, ...), condition=%wide.region_9.11_spmd.clone, body=%wide.region_5.10_spmd.clone.sunk | while | flops 3156385280 | bytes 104405952 | solution.py:147
  604.3 62.1 %all-gather.13.cloned.1.call-done = f32[5120,128]{1,0:T(8,128)} async-done(((f32[40,128]{1,0:T(8,128)}), f32[5120,128]{1,0:T(8,128)}) %all-gather.13.cloned.1.call-update) | async-done | bytes 2621456 | tf_op jit(solution)/shard_map/while/body/eval_jaxpr/all_gather | solution.py:137
  670.4 14.4 %fusion.93 = f32[128,25,1024]{2,0,1:T(8,128)S(1)} fusion(f32[40,25,1024]{2,0,1:T(8,128)} %get-tuple-element.816, f32[40,128]{1,0:T(8,128)S(1)} %reduce_sum.114, f32[128]{0:T(128)S(1)} %get-tuple-element.738, f32[128]{0:T(128)S(1)} %get-tuple-element.737), kind=kOutput, calls=%fused_computation.70.clone.1 | convolution fusion | flops 1572874240 | bytes 17224704 | tf_op jit(solution)/shard_map/while/body/eval_jaxpr/mvc,mk->vck/dot_general | solution.py:96
  684.8 9.2 fusion.96
  712.4 62.1 %all-gather.13.cloned.1.call-done = f32[5120,128]{1,0:T(8,128)} async-done(((f32[40,128]{1,0:T(8,128)}), f32[5120,128]{1,0:T(8,128)}) %all-gather.13.cloned.1.call-update) | async-done | bytes 2621456 | tf_op jit(solution)/shard_map/while/body/eval_jaxpr/all_gather | solution.py:137
  778.5 14.4 %fusion.93 = f32[128,25,1024]{2,0,1:T(8,128)S(1)} fusion(f32[40,25,1024]{2,0,1:T(8,128)} %get-tuple-element.816, f32[40,128]{1,0:T(8,128)S(1)} %reduce_sum.114, f32[128]{0:T(128)S(1)} %get-tuple-element.738, f32[128]{0:T(128)S(1)} %get-tuple-element.737), kind=kOutput, calls=%fused_computation.70.clone.1 | convolution fusion | flops 1572874240 | bytes 17224704 | tf_op jit(solution)/shard_map/while/body/eval_jaxpr/mvc,mk->vck/dot_general | solution.py:96
  792.9 9.2 fusion.96
  820.5 62.1 %all-gather.13.cloned.1.call-done = f32[5120,128]{1,0:T(8,128)} async-done(((f32[40,128]{1,0:T(8,128)}), f32[5120,128]{1,0:T(8,128)}) %all-gather.13.cloned.1.call-update) | async-done | bytes 2621456 | tf_op jit(solution)/shard_map/while/body/eval_jaxpr/all_gather | solution.py:137
  886.6 14.4 %fusion.93 = f32[128,25,1024]{2,0,1:T(8,128)S(1)} fusion(f32[40,25,1024]{2,0,1:T(8,128)} %get-tuple-element.816, f32[40,128]{1,0:T(8,128)S(1)} %reduce_sum.114, f32[128]{0:T(128)S(1)} %get-tuple-element.738, f32[128]{0:T(128)S(1)} %get-tuple-element.737), kind=kOutput, calls=%fused_computation.70.clone.1 | convolution fusion | flops 1572874240 | bytes 17224704 | tf_op jit(solution)/shard_map/while/body/eval_jaxpr/mvc,mk->vck/dot_general | solution.py:96
  901.0 9.2 fusion.96
  928.6 62.1 %all-gather.13.cloned.1.call-done = f32[5120,128]{1,0:T(8,128)} async-done(((f32[40,128]{1,0:T(8,128)}), f32[5120,128]{1,0:T(8,128)}) %all-gather.13.cloned.1.call-update) | async-done | bytes 2621456 | tf_op jit(solution)/shard_map/while/body/eval_jaxpr/all_gather | solution.py:137
  994.8 14.4 %fusion.93 = f32[128,25,1024]{2,0,1:T(8,128)S(1)} fusion(f32[40,25,1024]{2,0,1:T(8,128)} %get-tuple-element.816, f32[40,128]{1,0:T(8,128)S(1)} %reduce_sum.114, f32[128]{0:T(128)S(1)} %get-tuple-element.738, f32[128]{0:T(128)S(1)} %get-tuple-element.737), kind=kOutput, calls=%fused_computation.70.clone.1 | convolution fusion | flops 1572874240 | bytes 17224704 | tf_op jit(solution)/shard_map/while/body/eval_jaxpr/mvc,mk->vck/dot_general | solution.py:96
  1009.2 9.2 fusion.96
  (233 shorter events, 257.4 us)
Async XLA Ops:
  10.7 13.6 %collective-permute-start = (f32[40,25,1,128]{3,0,2,1:T(8,128)S(1)}, f32[40,25,1,128]{3,0,2,1:T(8,128)S(1)}, u32[]{:S(2)}, u32[]{:S(2)}) collective-permute-start(f32[40,25,1,128]{3,0,2,1:T(8,128)S(1)} %copy.94), channel_id=1, source_target_pairs={{0,16},{16,32},{32,48},{48,64},{64,80},{80,96},{96,112},{112,0},{1... | collective-permute-start | bytes 1536008 | tf_op jit(solution)/shard_map/ppermute | solution.py:18
  14.1 9.6 copy-start.9
  14.1 10.2 copy-start.8
  14.1 12.1 %collective-permute-start.1 = (f32[40,25,1,128]{3,0,2,1:T(8,128)}, f32[40,25,1,128]{3,0,2,1:T(8,128)S(1)}, u32[]{:S(2)}, u32[]{:S(2)}) collective-permute-start(f32[40,25,1,128]{3,0,2,1:T(8,128)} %copy.95), channel_id=1, source_target_pairs={{16,0},{32,16},{48,32},{64,48},{80,64},{96,80},{112,96},{0,112},{1... | collective-permute-start | bytes 1536008 | tf_op jit(solution)/shard_map/ppermute | solution.py:21
  37.5 7.0 copy-start.6
  44.5 22.0 %collective-permute-start.2 = (f32[40,25,10,1]{0,1,3,2:T(8,128)S(1)}, f32[40,25,10,1]{0,1,3,2:T(8,128)S(1)}, u32[]{:S(2)}, u32[]{:S(2)}) collective-permute-start(f32[40,25,10,1]{0,1,3,2:T(8,128)S(1)} %get-tuple-element.569), channel_id=1, source_target_pairs={{0,1},{1,2},{2,3},{3,4},{4,5},{5,6},{6,7},{7,8},{8,9},{9,10},{10,1... | collective-permute-start | bytes 120008 | tf_op jit(solution)/shard_map/ppermute | solution.py:18
  45.9 24.1 %collective-permute-start.3 = (f32[40,25,10,1]{0,1,3,2:T(8,128)S(1)}, f32[40,25,10,1]{0,1,3,2:T(8,128)S(1)}, u32[]{:S(2)}, u32[]{:S(2)}) collective-permute-start(f32[40,25,10,1]{0,1,3,2:T(8,128)S(1)} %get-tuple-element.570), channel_id=1, source_target_pairs={{1,0},{2,1},{3,2},{4,3},{5,4},{6,5},{7,6},{8,7},{9,8},{10,9},{11,1... | collective-permute-start | bytes 120008 | tf_op jit(solution)/shard_map/ppermute | solution.py:21
  86.6 16.5 %copy-start.10 = (s32[2,512]{1,0:T(2,128)S(1)}, s32[2,512]{1,0:T(2,128)}, u32[]{:S(2)}) copy-start(s32[2,512]{1,0:T(2,128)} %param.15) | copy-start | bytes 12292
  86.6 16.6 %copy-start.11 = (s32[2,512]{1,0:T(2,128)S(1)}, s32[2,512]{1,0:T(2,128)}, u32[]{:S(2)}) copy-start(s32[2,512]{1,0:T(2,128)} %param.16) | copy-start | bytes 12292
  86.6 16.6 %copy-start.12 = (s32[2,512]{1,0:T(2,128)S(1)}, s32[2,512]{1,0:T(2,128)}, u32[]{:S(2)}) copy-start(s32[2,512]{1,0:T(2,128)} %param.17) | copy-start | bytes 12292
  100.9 11.3 %copy-start.7 = (f32[40,25,8,128]{3,0,2,1:T(8,128)}, f32[40,25,8,128]{3,0,2,1:T(8,128)S(1)}, u32[]{:S(2)}) copy-start(f32[40,25,8,128]{3,0,2,1:T(8,128)S(1)} %multiply_add_fusion.2) | copy-start | bytes 12288004
  101.0 8.0 collective-permute-start.4
  103.0 8.8 collective-permute-start.5
  117.8 13.4 %copy-start.13 = (f32[2,512]{1,0:T(2,128)S(1)}, f32[2,512]{1,0:T(2,128)}, u32[]{:S(2)}) copy-start(f32[2,512]{1,0:T(2,128)} %param.19) | copy-start | bytes 12292
  121.9 9.4 collective-permute-start.6
  126.0 8.6 collective-permute-start.7
  153.5 82.8 %all-gather.11.cloned.1.call-start = ((), (), s32[]{:S(2)}) async-start(), calls=%async_computation | async-start | bytes 2641920 | tf_op jit(solution)/shard_map/while/body/eval_jaxpr/all_gather | solution.py:137
  239.7 14.4 %copy-start = (f32[40,25,1024]{2,0,1:T(8,128)S(1)}, f32[40,25,1024]{2,0,1:T(8,128)}, u32[]{:S(2)}) copy-start(f32[40,25,1024]{2,0,1:T(8,128)} %get-tuple-element.762) | copy-start | bytes 12288004 | tf_op jit(solution)/shard_map/while
  265.2 78.5 %all-gather.11.cloned.1.call-start = ((), (), s32[]{:S(2)}) async-start(), calls=%async_computation | async-start | bytes 2641920 | tf_op jit(solution)/shard_map/while/body/eval_jaxpr/all_gather | solution.py:137
  347.1 14.4 %copy-start = (f32[40,25,1024]{2,0,1:T(8,128)S(1)}, f32[40,25,1024]{2,0,1:T(8,128)}, u32[]{:S(2)}) copy-start(f32[40,25,1024]{2,0,1:T(8,128)} %get-tuple-element.762) | copy-start | bytes 12288004 | tf_op jit(solution)/shard_map/while
  372.7 78.5 %all-gather.11.cloned.1.call-start = ((), (), s32[]{:S(2)}) async-start(), calls=%async_computation | async-start | bytes 2641920 | tf_op jit(solution)/shard_map/while/body/eval_jaxpr/all_gather | solution.py:137
  454.6 14.4 %copy-start = (f32[40,25,1024]{2,0,1:T(8,128)S(1)}, f32[40,25,1024]{2,0,1:T(8,128)}, u32[]{:S(2)}) copy-start(f32[40,25,1024]{2,0,1:T(8,128)} %get-tuple-element.762) | copy-start | bytes 12288004 | tf_op jit(solution)/shard_map/while
  480.1 78.5 %all-gather.11.cloned.1.call-start = ((), (), s32[]{:S(2)}) async-start(), calls=%async_computation | async-start | bytes 2641920 | tf_op jit(solution)/shard_map/while/body/eval_jaxpr/all_gather | solution.py:137
  562.0 14.4 %copy-start = (f32[40,25,1024]{2,0,1:T(8,128)S(1)}, f32[40,25,1024]{2,0,1:T(8,128)}, u32[]{:S(2)}) copy-start(f32[40,25,1024]{2,0,1:T(8,128)} %get-tuple-element.762) | copy-start | bytes 12288004 | tf_op jit(solution)/shard_map/while
  587.8 78.6 %all-gather.13.cloned.1.call-start = ((), (), s32[]{:S(2)}) async-start(), calls=%async_computation.1 | async-start | bytes 2641920 | tf_op jit(solution)/shard_map/while/body/eval_jaxpr/all_gather | solution.py:137
  670.4 14.4 %copy-start.2 = (f32[40,25,1024]{2,0,1:T(8,128)S(1)}, f32[40,25,1024]{2,0,1:T(8,128)}, u32[]{:S(2)}) copy-start(f32[40,25,1024]{2,0,1:T(8,128)} %get-tuple-element.816) | copy-start | bytes 12288004 | tf_op jit(solution)/shard_map/while
  696.0 78.5 %all-gather.13.cloned.1.call-start = ((), (), s32[]{:S(2)}) async-start(), calls=%async_computation.1 | async-start | bytes 2641920 | tf_op jit(solution)/shard_map/while/body/eval_jaxpr/all_gather | solution.py:137
  778.5 14.4 %copy-start.2 = (f32[40,25,1024]{2,0,1:T(8,128)S(1)}, f32[40,25,1024]{2,0,1:T(8,128)}, u32[]{:S(2)}) copy-start(f32[40,25,1024]{2,0,1:T(8,128)} %get-tuple-element.816) | copy-start | bytes 12288004 | tf_op jit(solution)/shard_map/while
  804.1 78.5 %all-gather.13.cloned.1.call-start = ((), (), s32[]{:S(2)}) async-start(), calls=%async_computation.1 | async-start | bytes 2641920 | tf_op jit(solution)/shard_map/while/body/eval_jaxpr/all_gather | solution.py:137
  886.6 14.4 %copy-start.2 = (f32[40,25,1024]{2,0,1:T(8,128)S(1)}, f32[40,25,1024]{2,0,1:T(8,128)}, u32[]{:S(2)}) copy-start(f32[40,25,1024]{2,0,1:T(8,128)} %get-tuple-element.816) | copy-start | bytes 12288004 | tf_op jit(solution)/shard_map/while
  912.2 78.5 %all-gather.13.cloned.1.call-start = ((), (), s32[]{:S(2)}) async-start(), calls=%async_computation.1 | async-start | bytes 2641920 | tf_op jit(solution)/shard_map/while/body/eval_jaxpr/all_gather | solution.py:137
  994.8 14.4 %copy-start.2 = (f32[40,25,1024]{2,0,1:T(8,128)S(1)}, f32[40,25,1024]{2,0,1:T(8,128)}, u32[]{:S(2)}) copy-start(f32[40,25,1024]{2,0,1:T(8,128)} %get-tuple-element.816) | copy-start | bytes 12288004 | tf_op jit(solution)/shard_map/while
  (16 other events, 36.1 us)
Sparse Core Ops, SparseCore 0:
  169.1 67.0 all-gather.10
  280.8 62.8 all-gather.10
  388.3 62.8 all-gather.10
  495.7 62.8 all-gather.10
  603.4 62.8 all-gather.12
  711.6 62.8 all-gather.12
  819.7 62.8 all-gather.12
  927.8 62.8 all-gather.12
